TPU v7x, 32 devices: a whole 2x2x4 slice. The times are simulated.
32 devices in a mesh: group: 2 (over x), seq: 8 (over z, y), tensor: 2 (over core).
Axes of the slice: x: 2, y: 2, z: 4, core: 2. Of those that a mesh axis runs over, the one named last changes fastest.
Arguments:
- hidden: bfloat16 [6, 1024, 8192], P('group', 'seq', 'tensor'), parts along dimension 0, may hold values from -64 to 64
- norm_gain: bfloat16 [8192], replicated, may hold values from 0.099609375 to 1.8984375
- w_kv: bfloat16 [8192, 1024], P(None, 'tensor'), may hold values from -0.0625 to 0.0625
- lengths: int32 [6], P('group'), parts along dimension 0, may hold values from 512 to 1024
- page_table: int32 [6, 8], P('group', 'seq'), parts along dimension 0, may hold values from 0 to 63, as said below
Outputs:
- kv_cache: bfloat16 [128, 128, 1024], P(('group', 'seq'), None, 'tensor'), parts along dimension 0
There are 2 independent parts, one for each index of `group`. A program takes and returns all parts, laid end to end along the dimension named above; an argument that names none is the same for every part. Nothing has to cross between parts.
Inputs may be any that keep to these rules, and one draw needn't show every extreme that they name: `page_table`: entries are distinct; page p is held by index p // 8 of seq in its slot p % 8. In every draw some index of seq holds 8 pages whose blocks all start below the window's length, and some index of seq sends all its 3 blocks to that one holder.
All inputs are finite; a program needn't handle non-finite values.
Results may differ from a plain program's by a relative error of at most 0.0049.
Values may be sent and summed in bfloat16 or wider, within the bound.
No kernel may reach another device: no remote copies, remote signals or barrier semaphores. Data moves between devices by JAX's collectives and lax.ppermute only.
A program may use at most 128 MiB of HBM per device.

v0:
```python
import functools

import jax
import jax.numpy as jnp
from jax import lax
from jax.experimental import pallas as pl
from jax.experimental.pallas import tpu as pltpu
from jax.sharding import PartitionSpec as P


HD = 128
BLOCK = 128
SLOTS = 8
LABEL_ROWS = 8
DEPTH = 512
VMEM_LIMIT = 16 << 20


epsilon = 1e-05
rope_base = 500000.0


def frequencies():
    index = jnp.arange(HD, dtype=jnp.int32).reshape(1, HD) % (HD // 2)
    return rope_base ** (-2.0 * index.astype(jnp.float32) / HD)


VMEM = pl.BlockSpec(memory_space=pltpu.VMEM)
SMEM = pl.BlockSpec(memory_space=pltpu.SMEM)
ANY = pl.BlockSpec(memory_space=pl.ANY)
HBM = pl.BlockSpec(memory_space=pltpu.HBM)


def near(array):
    return pltpu.with_memory_space_constraint(array, pltpu.VMEM)


def far_away(array):
    return pltpu.with_memory_space_constraint(array, pltpu.HBM)


def lane_squares(x):
    wide = x.astype(jnp.float32)
    wide = wide * wide
    total = wide[:, :128]
    for c in range(1, x.shape[1] // 128):
        total += wide[:, c * 128 : (c + 1) * 128]
    return total


def scaled_by(x, gain_ref, row):
    parts = []
    for c in range(x.shape[1] // 128):
        gain = gain_ref[pl.ds(row + c, 1), :]
        wide = x[:, c * 128 : (c + 1) * 128].astype(jnp.float32) * gain
        parts.append(wide.astype(jnp.bfloat16))
    return jnp.concatenate(parts, axis=1)


def first_half_kernel(row_count, x_hbm, g_hbm, w_hbm, freq_ref, acc_ref, sq_ref, far_ref, gain, cos_ref, sin_ref, *scratch):
    g_buf, x_buf, w_buf, x_sem, w_sem, sems = scratch
    width = x_hbm.shape[1]
    steps = width // DEPTH
    side = lax.axis_index("tensor")
    near_row = pl.multiple_of(side * width, width)
    far_row = pl.multiple_of((1 - side) * width, width)
    copies = []
    for k in range(steps):
        span = slice(k * DEPTH, (k + 1) * DEPTH)
        copies.append(
            (
                pltpu.make_async_copy(x_hbm.at[:, span], x_buf.at[:, span], x_sem.at[k]),
                pltpu.make_async_copy(
                    w_hbm.at[pl.ds(near_row + k * DEPTH, DEPTH)], w_buf.at[span], w_sem.at[k]
                ),
            )
        )
    far = pltpu.make_async_copy(w_hbm.at[pl.ds(far_row, width)], far_ref, sems.at[0])
    gain_copy = pltpu.make_async_copy(g_hbm, g_buf, sems.at[1])
    gain_copy.start()
    for x_copy, w_copy in copies:
        x_copy.start()
        w_copy.start()
    far.start()
    first = lax.axis_index("seq") * row_count
    position = first + lax.broadcasted_iota(jnp.int32, cos_ref.shape, 0)
    angle = position.astype(jnp.float32) * freq_ref[...]
    cos_ref[...] = jnp.cos(angle)
    sine = jnp.sin(angle)
    lane = lax.broadcasted_iota(jnp.int32, sine.shape, 1)
    sin_ref[...] = jnp.where(lane < HD // 2, -sine, sine)
    gain_copy.wait()
    gain[...] = g_buf[...].astype(jnp.float32)
    for k in range(steps):
        for copy in copies[k]:
            copy.wait()
        span = slice(k * DEPTH, (k + 1) * DEPTH)
        x = x_buf[:, span]
        scaled = scaled_by(x, gain, side * (width // 128) + k * (DEPTH // 128))
        part = jnp.dot(scaled, w_buf[span], preferred_element_type=jnp.float32)
        squares = lane_squares(x)
        if k == 0:
            acc_ref[...] = part
            sq_ref[...] = squares
        else:
            acc_ref[...] += part
            sq_ref[...] += squares
    far.wait()


def first_half(x, gain, w, freq, row_count):
    rows, width = x.shape
    cols = w.shape[1]
    steps = width // DEPTH
    return pl.pallas_call(
        functools.partial(first_half_kernel, row_count),
        in_specs=[HBM, HBM, HBM, VMEM],
        out_specs=[VMEM] * 6,
        out_shape=[
            pltpu.VMEM((rows, cols), jnp.float32),
            pltpu.VMEM((rows, 128), jnp.float32),
            pltpu.VMEM((width, cols), jnp.bfloat16),
            pltpu.VMEM(gain.shape, jnp.float32),
            pltpu.VMEM((row_count, HD), jnp.float32),
            pltpu.VMEM((row_count, HD), jnp.float32),
        ],
        scratch_shapes=[
            pltpu.VMEM(gain.shape, jnp.bfloat16),
            pltpu.VMEM((rows, width), jnp.bfloat16),
            pltpu.VMEM((width, cols), jnp.bfloat16),
            pltpu.SemaphoreType.DMA((steps,)),
            pltpu.SemaphoreType.DMA((steps,)),
            pltpu.SemaphoreType.DMA((2,)),
        ],
        compiler_params=pltpu.CompilerParams(vmem_limit_bytes=VMEM_LIMIT),
        cost_estimate=pl.CostEstimate(
            flops=2 * rows * width * cols,
            bytes_accessed=2 * (rows * width + 2 * width * cols) + 4 * rows * cols,
            transcendentals=0,
        ),
        name="first_half",
    )(far_away(x), far_away(gain), far_away(w), freq)


def labels_of(page_ref):
    lane = lax.broadcasted_iota(jnp.int32, (LABEL_ROWS, 128), 1)
    tile = jnp.zeros((LABEL_ROWS, 128), jnp.int32)
    for b in range(page_ref.shape[0]):
        tile = jnp.where(lane == 2 * b, page_ref[b] // SLOTS, tile)
        tile = jnp.where(lane == 2 * b + 1, page_ref[b] % SLOTS, tile)
    return tile.astype(jnp.float32).astype(jnp.bfloat16)


def second_half_kernel(group, members, len_ref, page_ref, x_ref, g_ref, w_ref, acc_in, sq_in, cos_ref, sin_ref, *outs):
    rows, width = x_ref.shape
    per_seq = cos_ref.shape[0]
    per = per_seq // BLOCK
    blocks = rows // BLOCK
    tiles = acc_in.shape[1] // 128
    chunk = BLOCK // group
    side = lax.axis_index("tensor")
    own_index = lax.axis_index("seq")
    own = lax.rem(own_index, group)

    def chunks(ref, columns):
        parts = []
        for m in members:
            for b in range(blocks):
                start = pl.multiple_of(b * BLOCK + (own ^ m) * chunk, chunk)
                parts.append(ref[pl.ds(start, chunk), columns])
        return jnp.concatenate(parts, axis=0)

    acc = chunks(acc_in, slice(None))
    squares = chunks(sq_in, slice(None))
    for k in range(width // DEPTH):
        span = slice(k * DEPTH, (k + 1) * DEPTH)
        x = chunks(x_ref, span)
        scaled = scaled_by(x, g_ref, (1 - side) * (width // 128) + k * (DEPTH // 128))
        acc += jnp.dot(scaled, w_ref[span, :], preferred_element_type=jnp.float32)
        squares += lane_squares(x)
    total = jnp.sum(squares, axis=-1, keepdims=True)
    inv = jnp.broadcast_to(lax.rsqrt(total / (2 * width) + epsilon), squares.shape)
    labels = labels_of(page_ref)
    for i, m in enumerate(members):
        for b in range(blocks):
            at = (i * blocks + b) * chunk
            band = slice(at, at + chunk)
            first = pl.multiple_of(b % per * BLOCK + (own ^ m) * chunk, chunk)
            row = own_index * per_seq + first + lax.broadcasted_iota(jnp.int32, (chunk, HD), 0)
            living = row < len_ref[b // per]
            cosine = cos_ref[pl.ds(first, chunk), :]
            sine = sin_ref[pl.ds(first, chunk), :]
            for tile in range(tiles):
                made = acc[band, tile * HD : (tile + 1) * HD] * inv[band]
                if tile % 2 == 0:
                    made = made * cosine + pltpu.roll(made, HD // 2, 1) * sine
                made = jnp.where(living, made, 0.0).astype(jnp.bfloat16)
                to = (b * tiles + tile) * chunk
                outs[i][to : to + chunk, :] = made
        outs[i][-LABEL_ROWS:, :] = labels


def second_half(lengths, pages, x, gain, w, acc, squares, cosine, sine, group, members):
    rows, width = x.shape
    cols = w.shape[1]
    height = rows // group * (cols // 128) + LABEL_ROWS
    count = rows // group * len(members)
    operands = [near(array) for array in (x, gain, w, acc, squares, cosine, sine)]
    return pl.pallas_call(
        functools.partial(second_half_kernel, group, members),
        in_specs=[SMEM] * 2 + [VMEM] * len(operands),
        out_specs=[VMEM] * len(members),
        out_shape=[pltpu.VMEM((height, 128), jnp.bfloat16)] * len(members),
        compiler_params=pltpu.CompilerParams(vmem_limit_bytes=VMEM_LIMIT),
        cost_estimate=pl.CostEstimate(
            flops=2 * count * width * cols,
            bytes_accessed=2 * width * (count + cols) + 4 * count * cols,
            transcendentals=0,
        ),
    )(lengths, pages, *operands)


def route_kernel(count, group, blocks, *refs):
    parts = refs[:count]
    outs = refs[count : count + group]
    pool, label_buf, label_ref, table, sem = refs[count + group :]
    _, tiles, chunk, _ = pool.shape
    for k in range(count):
        label_buf[k : k + 1, :] = parts[k][-LABEL_ROWS:, :].astype(jnp.float32)[:1].astype(jnp.int32)
    copy = pltpu.make_async_copy(label_buf, label_ref, sem)
    copy.start()
    for k in range(count):
        for b in range(blocks):
            for tile in range(tiles):
                row = (b * tiles + tile) * chunk
                pool[k * blocks + b, tile] = parts[k][row : row + chunk, :]
    nothing = count * blocks
    pool[nothing] = jnp.zeros(pool.shape[1:], pool.dtype)
    wanted = group * SLOTS
    for i in range(wanted):
        table[i] = nothing
    copy.wait()
    own_index = lax.axis_index("seq")
    for k in range(count):
        for b in range(blocks):
            member = label_ref[k, 2 * b] ^ own_index
            slot = label_ref[k, 2 * b + 1]
            table[jnp.where(member < group, member * SLOTS + slot, wanted)] = k * blocks + b
    for m in range(group):
        for s in range(SLOTS):
            outs[m][s] = pool[table[m * SLOTS + s]]


def route(parts, group, blocks):
    count = len(parts)
    chunk = BLOCK // group
    tiles = (parts[0].shape[0] - LABEL_ROWS) // (blocks * chunk)
    return pl.pallas_call(
        functools.partial(route_kernel, count, group, blocks),
        in_specs=[VMEM] * count,
        out_specs=[VMEM] * group,
        out_shape=[pltpu.VMEM((SLOTS, tiles, chunk, 128), jnp.bfloat16)] * group,
        scratch_shapes=[
            pltpu.VMEM((count * blocks + 1, tiles, chunk, 128), jnp.bfloat16),
            pltpu.VMEM((count, 128), jnp.int32),
            pltpu.SMEM((count, 128), jnp.int32),
            pltpu.SMEM((group * SLOTS + 1,), jnp.int32),
            pltpu.SemaphoreType.DMA,
        ],
        compiler_params=pltpu.CompilerParams(vmem_limit_bytes=VMEM_LIMIT),
        cost_estimate=pl.CostEstimate(
            flops=0,
            bytes_accessed=256 * (count * blocks + group * SLOTS) * tiles * chunk,
            transcendentals=0,
        ),
        name="route",
    )(*[near(part) for part in parts])


def join_kernel(members, *refs):
    out, sems = refs[-2:]
    parts = refs[: len(members)]
    _, tiles, chunk, _ = parts[0].shape
    own = lax.rem(lax.axis_index("seq"), BLOCK // chunk)
    copies = []
    for at, m in enumerate(members):
        start = pl.multiple_of((own ^ m) * chunk, chunk)
        for tile in range(tiles):
            there = out.at[:, pl.ds(start, chunk), tile * 128 : (tile + 1) * 128]
            copy = pltpu.make_async_copy(parts[at].at[:, tile], there, sems.at[at, tile])
            copy.start()
            copies.append(copy)
    for copy in copies:
        copy.wait()


def join(parts, members, before=None):
    slots, tiles, chunk, _ = parts[0].shape
    cols = tiles * 128
    operands = [near(part) for part in parts]
    in_specs = [VMEM] * len(parts)
    alias = {}
    if before is not None:
        operands.append(before)
        in_specs.append(ANY)
        alias = {len(parts): 0}
    return pl.pallas_call(
        functools.partial(join_kernel, members),
        in_specs=in_specs,
        out_specs=ANY,
        out_shape=jax.ShapeDtypeStruct((slots, BLOCK, cols), jnp.bfloat16),
        scratch_shapes=[pltpu.SemaphoreType.DMA((len(parts), tiles))],
        input_output_aliases=alias,
        compiler_params=pltpu.CompilerParams(vmem_limit_bytes=VMEM_LIMIT),
        cost_estimate=pl.CostEstimate(
            flops=0, bytes_accessed=4 * len(parts) * slots * chunk * cols, transcendentals=0
        ),
        name="join" if before is None else "join_last",
    )(*operands)


def per_device(seq_size, hidden, norm_gain, w_kv, lengths, page_table):
    seq_count, row_count, local_width = hidden.shape
    group = min(4, seq_size)
    flat = hidden.reshape(seq_count * row_count, local_width)
    other = lax.ppermute(flat, "tensor", [(0, 1), (1, 0)])

    def swap(array, k):
        return lax.ppermute(array, "seq", [(i, i ^ k) for i in range(seq_size)])

    gain = norm_gain.reshape(-1, 128)
    pages = page_table.reshape(-1)
    freq = frequencies()
    flat, freq = lax.optimization_barrier((flat, freq))
    acc, squares, far, gain, cosine, sine = first_half(flat, gain, w_kv, freq, row_count)
    outs = []

    def send(k):
        return swap(outs[k % group], k)

    shared = (lengths, pages, other, gain, far, acc, squares, cosine, sine, group)
    outs += second_half(*shared, (0,))
    parts = {k: send(k) for k in range(group, seq_size, group)}
    for members in (tuple(range(1, group)),):
        outs += second_half(*shared, members)
    parts[0] = outs[0]
    for k in range(1, seq_size):
        if k % group:
            parts[k] = send(k)
    sent = route([parts[k] for k in range(seq_size)], group, seq_count * row_count // BLOCK)
    placed = [sent[0]]
    for m in range(1, group):
        placed.append(swap(sent[m], m))
    members = tuple(range(group))
    kv_cache = join(placed[:-1], members[:-1])
    return join(placed[-1:], members[-1:], kv_cache)


def solution(mesh):
    placed = (P("group", "seq", "tensor"), P(), P(None, "tensor"), P("group"), P("group", "seq"))

    def body(*operands):
        return per_device(mesh.shape["seq"], *operands)

    return jax.shard_map(
        body,
        mesh=mesh,
        in_specs=placed,
        out_specs=P(("group", "seq"), None, "tensor"),
        check_vma=False,
    )
```

profile of v0, /device:TPU:0, one launch (start us, length us, event | category | flops | bytes accessed | tf_op | source)
XLA Modules:
  0.0 48.0 jit_solution(3137816203357952627)
XLA Ops:
  0.0 0.5 %collective-permute-start = (bf16[384,4096]{1,0:T(8,128)(2,1)}, bf16[384,4096]{1,0:T(8,128)(2,1)S(1)}, u32[]{:S(2)}, u32[]{:S(2)}) collective-permute-start(bf16[384,4096]{1,0:T(8,128)(2,1)} %bitcast.5), channel_id=1, source_target_pairs={{0,1},{1,0},{2,3},{3,2},{4,5},{5,4},{6,7},{7,6},{8,9},{9,8},{10,11... | collective-permute-start | bytes 9437192 | tf_op jit(solution)/shard_map/ppermute | solution.py:326
  0.5 0.0 copy-start.1
  0.5 5.0 %first_half.1 = (f32[384,512]{1,0:T(8,128)S(1)}, f32[384,128]{1,0:T(8,128)S(1)}, bf16[4096,512]{1,0:T(8,128)(2,1)S(1)}, f32[64,128]{1,0:T(8,128)S(1)}, f32[128,128]{1,0:T(8,128)S(1)}, /*index=5*/f32[128,128]{1,0:T(8,128)S(1)}) custom-call(bf16[384,4096]{1,0:T(8,128)(2,1)} %bitcast.6, bf16[64,128]{1,0:T(8,128)(2,1)} %bitcast.7, bf16[8192,512]{1,0:T(8,128)(2,1)} %w_hbm.1, ...), custom_call_target="tpu_custom_call" | custom-call | flops 1610612736 | bytes 12320768 | tf_op jit(solution)/shard_map/first_half/pallas_call | solution.py:115
  5.5 0.5 collective-permute-done.x_ref
  6.0 2.1 %shard_map.56 = (bf16[392,128]{1,0:T(8,128)(2,1)S(1)}, bf16[392,128]{1,0:T(8,128)(2,1)S(1)}, bf16[392,128]{1,0:T(8,128)(2,1)S(1)}) custom-call(s32[3]{0:T(128)S(1)} %copy-done, s32[3]{0:T(128)S(1)} %bitcast.3, bf16[384,4096]{1,0:T(8,128)(2,1)S(1)} %collective-permute-done.x_ref, f32[64,128]{1,0:T(8,128)S(1)} %get-tuple-element.22.g_ref, ...), custom_call_target="tpu_custom_call" | custom-call | flops 1207959552 | bytes 7143424 | tf_op jit(solution)/shard_map/pallas_call | solution.py:209
  8.1 5.0 %collective-permute-start.5 = (bf16[392,128]{1,0:T(8,128)(2,1)S(1)}, bf16[392,128]{1,0:T(8,128)(2,1)S(1)}, u32[]{:S(2)}, u32[]{:S(2)}) collective-permute-start(bf16[392,128]{1,0:T(8,128)(2,1)S(1)} %get-tuple-element.28), channel_id=1, source_target_pairs={{0,10},{2,8},{4,14},{6,12},{8,2},{10,0},{12,6},{14,4},{1,11},{3,9}... | collective-permute-start | bytes 301064 | tf_op jit(solution)/shard_map/ppermute | solution.py:329
  13.1 0.5 %collective-permute-start.1 = (bf16[392,128]{1,0:T(8,128)(2,1)S(1)}, bf16[392,128]{1,0:T(8,128)(2,1)S(1)}, u32[]{:S(2)}, u32[]{:S(2)}) collective-permute-start(bf16[392,128]{1,0:T(8,128)(2,1)S(1)} %get-tuple-element.28), channel_id=1, source_target_pairs={{0,2},{2,0},{4,6},{6,4},{8,10},{10,8},{12,14},{14,12},{1,3},{3,1},... | collective-permute-start | bytes 301064 | tf_op jit(solution)/shard_map/ppermute | solution.py:329
  13.6 1.3 %collective-permute-start.6 = (bf16[392,128]{1,0:T(8,128)(2,1)S(1)}, bf16[392,128]{1,0:T(8,128)(2,1)S(1)}, u32[]{:S(2)}, u32[]{:S(2)}) collective-permute-start(bf16[392,128]{1,0:T(8,128)(2,1)S(1)} %get-tuple-element.29), channel_id=1, source_target_pairs={{0,12},{2,14},{4,8},{6,10},{8,4},{10,6},{12,0},{14,2},{1,13},{3,15... | collective-permute-start | bytes 301064 | tf_op jit(solution)/shard_map/ppermute | solution.py:329
  15.0 0.2 collective-permute-start.2
  15.2 3.9 %collective-permute-start.7 = (bf16[392,128]{1,0:T(8,128)(2,1)S(1)}, bf16[392,128]{1,0:T(8,128)(2,1)S(1)}, u32[]{:S(2)}, u32[]{:S(2)}) collective-permute-start(bf16[392,128]{1,0:T(8,128)(2,1)S(1)} %get-tuple-element.30), channel_id=1, source_target_pairs={{0,14},{2,12},{4,10},{6,8},{8,6},{10,4},{12,2},{14,0},{1,15},{3,13... | collective-permute-start | bytes 301064 | tf_op jit(solution)/shard_map/ppermute | solution.py:329
  19.1 1.4 %shard_map.55.refs_0_ = bf16[392,128]{1,0:T(8,128)(2,1)S(1)} custom-call(s32[3]{0:T(128)S(1)} %copy-done, s32[3]{0:T(128)S(1)} %bitcast.4, bf16[384,4096]{1,0:T(8,128)(2,1)S(1)} %collective-permute-done.x_ref, f32[64,128]{1,0:T(8,128)S(1)} %get-tuple-element.22.g_ref, bf16[4096,512]{1,0:T(8,128)(2,1)S(1)} %get-tuple-element.23.w_ref, ...), custom_call_target="tpu_custom_call" | custom-call | flops 402653184 | bytes 5177344 | tf_op jit(solution)/shard_map/pallas_call | solution.py:209
  20.5 1.8 %collective-permute-start.3 = (bf16[392,128]{1,0:T(8,128)(2,1)S(1)}, bf16[392,128]{1,0:T(8,128)(2,1)S(1)}, u32[]{:S(2)}, u32[]{:S(2)}) collective-permute-start(bf16[392,128]{1,0:T(8,128)(2,1)S(1)} %get-tuple-element.30), channel_id=1, source_target_pairs={{0,6},{2,4},{4,2},{6,0},{8,14},{10,12},{12,10},{14,8},{1,7},{3,5},... | collective-permute-start | bytes 301064 | tf_op jit(solution)/shard_map/ppermute | solution.py:329
  22.4 4.1 %collective-permute-start.4 = (bf16[392,128]{1,0:T(8,128)(2,1)S(1)}, bf16[392,128]{1,0:T(8,128)(2,1)S(1)}, u32[]{:S(2)}, u32[]{:S(2)}) collective-permute-start(bf16[392,128]{1,0:T(8,128)(2,1)S(1)} %shard_map.55.refs_0_), channel_id=1, source_target_pairs={{0,8},{2,10},{4,12},{6,14},{8,0},{10,2},{12,4},{14,6},{1,9},{3,11}... | collective-permute-start | bytes 301064 | tf_op jit(solution)/shard_map/ppermute | solution.py:329
  26.5 0.5 %collective-permute-done.3.refs_3_ = bf16[392,128]{1,0:T(8,128)(2,1)S(1)} collective-permute-done((bf16[392,128]{1,0:T(8,128)(2,1)S(1)}, bf16[392,128]{1,0:T(8,128)(2,1)S(1)}, u32[]{:S(2)}, u32[]{:S(2)}) %collective-permute-start.3) | collective-permute-done | bytes 100384 | tf_op jit(solution)/shard_map/ppermute | solution.py:329
  27.0 4.8 %collective-permute-done.4.refs_4_ = bf16[392,128]{1,0:T(8,128)(2,1)S(1)} collective-permute-done((bf16[392,128]{1,0:T(8,128)(2,1)S(1)}, bf16[392,128]{1,0:T(8,128)(2,1)S(1)}, u32[]{:S(2)}, u32[]{:S(2)}) %collective-permute-start.4) | collective-permute-done | bytes 100384 | tf_op jit(solution)/shard_map/ppermute | solution.py:329
  31.8 0.8 %route.1 = (bf16[8,4,32,128]{3,2,1,0:T(8,128)(2,1)S(1)}, bf16[8,4,32,128]{3,2,1,0:T(8,128)(2,1)S(1)}, bf16[8,4,32,128]{3,2,1,0:T(8,128)(2,1)S(1)}, bf16[8,4,32,128]{3,2,1,0:T(8,128)(2,1)S(1)}) custom-call(bf16[392,128]{1,0:T(8,128)(2,1)S(1)} %shard_map.55.refs_0_, bf16[392,128]{1,0:T(8,128)(2,1)S(1)} %collective-permute-done.1.refs_1_, ...), custom_call_target="tpu_custom_call" | custom-call | bytes 1835008 | tf_op jit(solution)/shard_map/route/pallas_call | solution.py:258
  32.5 0.4 collective-permute-start.9
  33.0 1.1 %collective-permute-start.10 = (bf16[8,4,32,128]{3,2,1,0:T(8,128)(2,1)S(1)}, bf16[8,4,32,128]{3,2,1,0:T(8,128)(2,1)S(1)}, u32[]{:S(2)}, u32[]{:S(2)}) collective-permute-start(bf16[8,4,32,128]{3,2,1,0:T(8,128)(2,1)S(1)} %get-tuple-element.34), channel_id=1, source_target_pairs={{0,4},{2,6},{4,0},{6,2},{8,12},{10,14},{12,8},{14,10},{1,5},{3,7},... | collective-permute-start | bytes 786440 | tf_op jit(solution)/shard_map/ppermute | solution.py:329
  34.1 2.0 %collective-permute-start.8 = (bf16[8,4,32,128]{3,2,1,0:T(8,128)(2,1)S(1)}, bf16[8,4,32,128]{3,2,1,0:T(8,128)(2,1)S(1)}, u32[]{:S(2)}, u32[]{:S(2)}) collective-permute-start(bf16[8,4,32,128]{3,2,1,0:T(8,128)(2,1)S(1)} %get-tuple-element.31), channel_id=1, source_target_pairs={{0,6},{2,4},{4,2},{6,0},{8,14},{10,12},{12,10},{14,8},{1,7},{3,5},... | collective-permute-start | bytes 786440 | tf_op jit(solution)/shard_map/ppermute | solution.py:329
  36.1 4.8 %collective-permute-done.9.refs_1_ = bf16[8,4,32,128]{3,2,1,0:T(8,128)(2,1)S(1)} collective-permute-done((bf16[8,4,32,128]{3,2,1,0:T(8,128)(2,1)S(1)}, bf16[8,4,32,128]{3,2,1,0:T(8,128)(2,1)S(1)}, u32[]{:S(2)}, u32[]{:S(2)}) %collective-permute-start.9) | collective-permute-done | bytes 262176 | tf_op jit(solution)/shard_map/ppermute | solution.py:329
  40.9 1.3 %collective-permute-done.10.refs_2_ = bf16[8,4,32,128]{3,2,1,0:T(8,128)(2,1)S(1)} collective-permute-done((bf16[8,4,32,128]{3,2,1,0:T(8,128)(2,1)S(1)}, bf16[8,4,32,128]{3,2,1,0:T(8,128)(2,1)S(1)}, u32[]{:S(2)}, u32[]{:S(2)}) %collective-permute-start.10) | collective-permute-done | bytes 262176 | tf_op jit(solution)/shard_map/ppermute | solution.py:329
  42.2 1.0 %join.1.refs_1_ = bf16[8,128,512]{2,1,0:T(8,128)(2,1)} custom-call(bf16[8,4,32,128]{3,2,1,0:T(8,128)(2,1)S(1)} %get-tuple-element.32.refs_0_, bf16[8,4,32,128]{3,2,1,0:T(8,128)(2,1)S(1)} %collective-permute-done.9.refs_1_, bf16[8,4,32,128]{3,2,1,0:T(8,128)(2,1)S(1)} %collective-permute-done.10.refs_2_), custom_call_target="tpu_custom_call" | custom-call | bytes 1572864 | tf_op jit(solution)/shard_map/join/pallas_call | solution.py:307
  43.1 4.1 %collective-permute-done.8.refs_0_ = bf16[8,4,32,128]{3,2,1,0:T(8,128)(2,1)S(1)} collective-permute-done((bf16[8,4,32,128]{3,2,1,0:T(8,128)(2,1)S(1)}, bf16[8,4,32,128]{3,2,1,0:T(8,128)(2,1)S(1)}, u32[]{:S(2)}, u32[]{:S(2)}) %collective-permute-start.8) | collective-permute-done | bytes 262176 | tf_op jit(solution)/shard_map/ppermute | solution.py:329
  47.3 0.7 %join_last.1 = bf16[8,128,512]{2,1,0:T(8,128)(2,1)} custom-call(bf16[8,4,32,128]{3,2,1,0:T(8,128)(2,1)S(1)} %collective-permute-done.8.refs_0_, bf16[8,128,512]{2,1,0:T(8,128)(2,1)} %join.1.refs_1_), custom_call_target="tpu_custom_call", output_to_operand_aliasing={{}: (1, {})} | custom-call | bytes 524288 | tf_op jit(solution)/shard_map/join_last/pallas_call | solution.py:307
  (9 shorter events, 0.0 us)
Async XLA Ops:
  0.0 6.0 %collective-permute-start = (bf16[384,4096]{1,0:T(8,128)(2,1)}, bf16[384,4096]{1,0:T(8,128)(2,1)S(1)}, u32[]{:S(2)}, u32[]{:S(2)}) collective-permute-start(bf16[384,4096]{1,0:T(8,128)(2,1)} %bitcast.5), channel_id=1, source_target_pairs={{0,1},{1,0},{2,3},{3,2},{4,5},{5,4},{6,7},{7,6},{8,9},{9,8},{10,11... | collective-permute-start | bytes 9437192 | tf_op jit(solution)/shard_map/ppermute | solution.py:326
  0.5 5.5 %copy-start = (s32[3]{0:T(128)S(1)}, s32[3]{0:T(128)}, u32[]{:S(2)}) copy-start(s32[3]{0:T(128)} %len_ref.3) | copy-start | bytes 40
  0.5 5.5 %copy-start.1 = (s32[3,1]{0,1:T(1,128)S(1)}, s32[3,1]{0,1:T(1,128)}, u32[]{:S(2)}) copy-start(s32[3,1]{0,1:T(1,128)} %param.9) | copy-start | bytes 40
  8.1 12.4 %collective-permute-start.5 = (bf16[392,128]{1,0:T(8,128)(2,1)S(1)}, bf16[392,128]{1,0:T(8,128)(2,1)S(1)}, u32[]{:S(2)}, u32[]{:S(2)}) collective-permute-start(bf16[392,128]{1,0:T(8,128)(2,1)S(1)} %get-tuple-element.28), channel_id=1, source_target_pairs={{0,10},{2,8},{4,14},{6,12},{8,2},{10,0},{12,6},{14,4},{1,11},{3,9}... | collective-permute-start | bytes 301064 | tf_op jit(solution)/shard_map/ppermute | solution.py:329
  13.1 9.3 %collective-permute-start.1 = (bf16[392,128]{1,0:T(8,128)(2,1)S(1)}, bf16[392,128]{1,0:T(8,128)(2,1)S(1)}, u32[]{:S(2)}, u32[]{:S(2)}) collective-permute-start(bf16[392,128]{1,0:T(8,128)(2,1)S(1)} %get-tuple-element.28), channel_id=1, source_target_pairs={{0,2},{2,0},{4,6},{6,4},{8,10},{10,8},{12,14},{14,12},{1,3},{3,1},... | collective-permute-start | bytes 301064 | tf_op jit(solution)/shard_map/ppermute | solution.py:329
  13.6 12.8 %collective-permute-start.6 = (bf16[392,128]{1,0:T(8,128)(2,1)S(1)}, bf16[392,128]{1,0:T(8,128)(2,1)S(1)}, u32[]{:S(2)}, u32[]{:S(2)}) collective-permute-start(bf16[392,128]{1,0:T(8,128)(2,1)S(1)} %get-tuple-element.29), channel_id=1, source_target_pairs={{0,12},{2,14},{4,8},{6,10},{8,4},{10,6},{12,0},{14,2},{1,13},{3,15... | collective-permute-start | bytes 301064 | tf_op jit(solution)/shard_map/ppermute | solution.py:329
  15.0 11.5 %collective-permute-start.2 = (bf16[392,128]{1,0:T(8,128)(2,1)S(1)}, bf16[392,128]{1,0:T(8,128)(2,1)S(1)}, u32[]{:S(2)}, u32[]{:S(2)}) collective-permute-start(bf16[392,128]{1,0:T(8,128)(2,1)S(1)} %get-tuple-element.29), channel_id=1, source_target_pairs={{0,4},{2,6},{4,0},{6,2},{8,12},{10,14},{12,8},{14,10},{1,5},{3,7},... | collective-permute-start | bytes 301064 | tf_op jit(solution)/shard_map/ppermute | solution.py:329
  15.2 11.3 %collective-permute-start.7 = (bf16[392,128]{1,0:T(8,128)(2,1)S(1)}, bf16[392,128]{1,0:T(8,128)(2,1)S(1)}, u32[]{:S(2)}, u32[]{:S(2)}) collective-permute-start(bf16[392,128]{1,0:T(8,128)(2,1)S(1)} %get-tuple-element.30), channel_id=1, source_target_pairs={{0,14},{2,12},{4,10},{6,8},{8,6},{10,4},{12,2},{14,0},{1,15},{3,13... | collective-permute-start | bytes 301064 | tf_op jit(solution)/shard_map/ppermute | solution.py:329
  20.5 6.5 %collective-permute-start.3 = (bf16[392,128]{1,0:T(8,128)(2,1)S(1)}, bf16[392,128]{1,0:T(8,128)(2,1)S(1)}, u32[]{:S(2)}, u32[]{:S(2)}) collective-permute-start(bf16[392,128]{1,0:T(8,128)(2,1)S(1)} %get-tuple-element.30), channel_id=1, source_target_pairs={{0,6},{2,4},{4,2},{6,0},{8,14},{10,12},{12,10},{14,8},{1,7},{3,5},... | collective-permute-start | bytes 301064 | tf_op jit(solution)/shard_map/ppermute | solution.py:329
  22.4 9.4 %collective-permute-start.4 = (bf16[392,128]{1,0:T(8,128)(2,1)S(1)}, bf16[392,128]{1,0:T(8,128)(2,1)S(1)}, u32[]{:S(2)}, u32[]{:S(2)}) collective-permute-start(bf16[392,128]{1,0:T(8,128)(2,1)S(1)} %shard_map.55.refs_0_), channel_id=1, source_target_pairs={{0,8},{2,10},{4,12},{6,14},{8,0},{10,2},{12,4},{14,6},{1,9},{3,11}... | collective-permute-start | bytes 301064 | tf_op jit(solution)/shard_map/ppermute | solution.py:329
  32.5 8.3 %collective-permute-start.9 = (bf16[8,4,32,128]{3,2,1,0:T(8,128)(2,1)S(1)}, bf16[8,4,32,128]{3,2,1,0:T(8,128)(2,1)S(1)}, u32[]{:S(2)}, u32[]{:S(2)}) collective-permute-start(bf16[8,4,32,128]{3,2,1,0:T(8,128)(2,1)S(1)} %get-tuple-element.33), channel_id=1, source_target_pairs={{0,2},{2,0},{4,6},{6,4},{8,10},{10,8},{12,14},{14,12},{1,3},{3,1},... | collective-permute-start | bytes 786440 | tf_op jit(solution)/shard_map/ppermute | solution.py:329
  33.0 9.2 %collective-permute-start.10 = (bf16[8,4,32,128]{3,2,1,0:T(8,128)(2,1)S(1)}, bf16[8,4,32,128]{3,2,1,0:T(8,128)(2,1)S(1)}, u32[]{:S(2)}, u32[]{:S(2)}) collective-permute-start(bf16[8,4,32,128]{3,2,1,0:T(8,128)(2,1)S(1)} %get-tuple-element.34), channel_id=1, source_target_pairs={{0,4},{2,6},{4,0},{6,2},{8,12},{10,14},{12,8},{14,10},{1,5},{3,7},... | collective-permute-start | bytes 786440 | tf_op jit(solution)/shard_map/ppermute | solution.py:329
  34.1 13.2 %collective-permute-start.8 = (bf16[8,4,32,128]{3,2,1,0:T(8,128)(2,1)S(1)}, bf16[8,4,32,128]{3,2,1,0:T(8,128)(2,1)S(1)}, u32[]{:S(2)}, u32[]{:S(2)}) collective-permute-start(bf16[8,4,32,128]{3,2,1,0:T(8,128)(2,1)S(1)} %get-tuple-element.31), channel_id=1, source_target_pairs={{0,6},{2,4},{4,2},{6,0},{8,14},{10,12},{12,10},{14,8},{1,7},{3,5},... | collective-permute-start | bytes 786440 | tf_op jit(solution)/shard_map/ppermute | solution.py:329
where the time goes:
time: 48.1 us; the launch traced here: 48 us
  starting transfers between devices  20.9 us (43%)
  waiting for transfers between devices  15.9 us (33%)
  Pallas kernels  11 us (23%)
    ppermute x10, starting transfers between devices, swap(): return lax.ppermute(array, 'seq', [(i, i ^ k) for i in range(seq_size)])  20.4 us
    ppermute x10, waiting for transfers between devices, swap(): return lax.ppermute(array, 'seq', [(i, i ^ k) for i in range(seq_size)])  15.5 us
    pallas_call x1, Pallas kernels, first_half(): pl.pallas_call(functools.partial(first_half_kernel, row_count), in_specs=...  5.01 us
    pallas_call x2, Pallas kernels, second_half(): pl.pallas_call(functools.partial(second_half_kernel, group, members), in_...  3.57 us
    pallas_call x2, Pallas kernels, join(): pl.pallas_call(functools.partial(join_kernel, members), in_specs=in_specs...  1.69 us
  transfers between devices with their start and end apart: 11, of which 6 were waited for; matrix products, arithmetic and copies ran while one was open for 0% of the time, Pallas kernels for 15%

commit v1 on v0

--- a/solution.py
+++ b/solution.py
@@ -143,11 +143,12 @@
 
 
 def labels_of(page_ref):
+    row = lax.broadcasted_iota(jnp.int32, (LABEL_ROWS, 128), 0)
     lane = lax.broadcasted_iota(jnp.int32, (LABEL_ROWS, 128), 1)
     tile = jnp.zeros((LABEL_ROWS, 128), jnp.int32)
     for b in range(page_ref.shape[0]):
-        tile = jnp.where(lane == 2 * b, page_ref[b] // SLOTS, tile)
-        tile = jnp.where(lane == 2 * b + 1, page_ref[b] % SLOTS, tile)
+        label = jnp.where(row == 0, page_ref[b] // SLOTS, page_ref[b] % SLOTS)
+        tile = jnp.where(lane == b, label, tile)
     return tile.astype(jnp.float32).astype(jnp.bfloat16)
 
 
@@ -223,12 +224,15 @@
 def route_kernel(count, group, blocks, *refs):
     parts = refs[:count]
     outs = refs[count : count + group]
-    pool, label_buf, label_ref, table, sem = refs[count + group :]
+    pool, table = refs[count + group :]
     _, tiles, chunk, _ = pool.shape
+    own_index = lax.axis_index("seq")
+    wanted = group * SLOTS
+    places = []
     for k in range(count):
-        label_buf[k : k + 1, :] = parts[k][-LABEL_ROWS:, :].astype(jnp.float32)[:1].astype(jnp.int32)
-    copy = pltpu.make_async_copy(label_buf, label_ref, sem)
-    copy.start()
+        label = parts[k][-LABEL_ROWS:, :].astype(jnp.float32).astype(jnp.int32)
+        member = label[0:1] ^ own_index
+        places.append(jnp.where(member < group, member * SLOTS + label[1:2], wanted))
     for k in range(count):
         for b in range(blocks):
             for tile in range(tiles):
@@ -236,16 +240,11 @@
                 pool[k * blocks + b, tile] = parts[k][row : row + chunk, :]
     nothing = count * blocks
     pool[nothing] = jnp.zeros(pool.shape[1:], pool.dtype)
-    wanted = group * SLOTS
     for i in range(wanted):
         table[i] = nothing
-    copy.wait()
-    own_index = lax.axis_index("seq")
     for k in range(count):
         for b in range(blocks):
-            member = label_ref[k, 2 * b] ^ own_index
-            slot = label_ref[k, 2 * b + 1]
-            table[jnp.where(member < group, member * SLOTS + slot, wanted)] = k * blocks + b
+            table[places[k][0, b]] = k * blocks + b
     for m in range(group):
         for s in range(SLOTS):
             outs[m][s] = pool[table[m * SLOTS + s]]
@@ -262,10 +261,7 @@
         out_shape=[pltpu.VMEM((SLOTS, tiles, chunk, 128), jnp.bfloat16)] * group,
         scratch_shapes=[
             pltpu.VMEM((count * blocks + 1, tiles, chunk, 128), jnp.bfloat16),
-            pltpu.VMEM((count, 128), jnp.int32),
-            pltpu.SMEM((count, 128), jnp.int32),
             pltpu.SMEM((group * SLOTS + 1,), jnp.int32),
-            pltpu.SemaphoreType.DMA,
         ],
         compiler_params=pltpu.CompilerParams(vmem_limit_bytes=VMEM_LIMIT),
         cost_estimate=pl.CostEstimate(

time: 48.1 us -> 47.6 us (0.990)
  Pallas kernels: 11 us -> 10.5 us
    pallas_call x1, Pallas kernels: 0.76 us -> 0.23 us  [route(): pl.pallas_call(functools.partial(route_kernel, count, group, blocks), in_...]
  transfers between devices with their start and end apart: 11 -> 11, of which waited for: 6 -> 6; matrix products, arithmetic and copies ran while one was open for 0% -> 0% of each run, Pallas kernels for 15% -> 16%
where the time goes in v1:
time: 47.6 us; the launch traced here: 47.5 us
  starting transfers between devices  20.9 us (44%)
  waiting for transfers between devices  15.9 us (33%)
  Pallas kernels  10.5 us (22%)
    ppermute x10, starting transfers between devices, swap(): return lax.ppermute(array, 'seq', [(i, i ^ k) for i in range(seq_size)])  20.4 us
    ppermute x10, waiting for transfers between devices, swap(): return lax.ppermute(array, 'seq', [(i, i ^ k) for i in range(seq_size)])  15.5 us
    pallas_call x1, Pallas kernels, first_half(): pl.pallas_call(functools.partial(first_half_kernel, row_count), in_specs=...  5.01 us
    pallas_call x2, Pallas kernels, second_half(): pl.pallas_call(functools.partial(second_half_kernel, group, members), in_...  3.56 us
    pallas_call x2, Pallas kernels, join(): pl.pallas_call(functools.partial(join_kernel, members), in_specs=in_specs...  1.69 us
  transfers between devices with their start and end apart: 11, of which 6 were waited for; matrix products, arithmetic and copies ran while one was open for 0% of the time, Pallas kernels for 16%

profile of v1, /device:TPU:0, one launch (start us, length us, event | category | flops | bytes accessed | tf_op | source)
XLA Modules:
  0.0 47.5 jit_solution(15383722781445874995)
XLA Ops:
  0.0 0.5 %collective-permute-start = (bf16[384,4096]{1,0:T(8,128)(2,1)}, bf16[384,4096]{1,0:T(8,128)(2,1)S(1)}, u32[]{:S(2)}, u32[]{:S(2)}) collective-permute-start(bf16[384,4096]{1,0:T(8,128)(2,1)} %bitcast.5), channel_id=1, source_target_pairs={{0,1},{1,0},{2,3},{3,2},{4,5},{5,4},{6,7},{7,6},{8,9},{9,8},{10,11... | collective-permute-start | bytes 9437192 | tf_op jit(solution)/shard_map/ppermute | solution.py:322
  0.5 0.0 copy-start.1
  0.5 5.0 %first_half.1 = (f32[384,512]{1,0:T(8,128)S(1)}, f32[384,128]{1,0:T(8,128)S(1)}, bf16[4096,512]{1,0:T(8,128)(2,1)S(1)}, f32[64,128]{1,0:T(8,128)S(1)}, f32[128,128]{1,0:T(8,128)S(1)}, /*index=5*/f32[128,128]{1,0:T(8,128)S(1)}) custom-call(bf16[384,4096]{1,0:T(8,128)(2,1)} %bitcast.6, bf16[64,128]{1,0:T(8,128)(2,1)} %bitcast.7, bf16[8192,512]{1,0:T(8,128)(2,1)} %w_hbm.1, ...), custom_call_target="tpu_custom_call" | custom-call | flops 1610612736 | bytes 12320768 | tf_op jit(solution)/shard_map/first_half/pallas_call | solution.py:115
  5.5 0.5 collective-permute-done.x_ref
  6.0 2.1 %shard_map.56 = (bf16[392,128]{1,0:T(8,128)(2,1)S(1)}, bf16[392,128]{1,0:T(8,128)(2,1)S(1)}, bf16[392,128]{1,0:T(8,128)(2,1)S(1)}) custom-call(s32[3]{0:T(128)S(1)} %copy-done, s32[3]{0:T(128)S(1)} %bitcast.3, bf16[384,4096]{1,0:T(8,128)(2,1)S(1)} %collective-permute-done.x_ref, f32[64,128]{1,0:T(8,128)S(1)} %get-tuple-element.22.g_ref, ...), custom_call_target="tpu_custom_call" | custom-call | flops 1207959552 | bytes 7143424 | tf_op jit(solution)/shard_map/pallas_call | solution.py:210
  8.1 5.0 %collective-permute-start.5 = (bf16[392,128]{1,0:T(8,128)(2,1)S(1)}, bf16[392,128]{1,0:T(8,128)(2,1)S(1)}, u32[]{:S(2)}, u32[]{:S(2)}) collective-permute-start(bf16[392,128]{1,0:T(8,128)(2,1)S(1)} %get-tuple-element.28), channel_id=1, source_target_pairs={{0,10},{2,8},{4,14},{6,12},{8,2},{10,0},{12,6},{14,4},{1,11},{3,9}... | collective-permute-start | bytes 301064 | tf_op jit(solution)/shard_map/ppermute | solution.py:325
  13.1 0.5 %collective-permute-start.1 = (bf16[392,128]{1,0:T(8,128)(2,1)S(1)}, bf16[392,128]{1,0:T(8,128)(2,1)S(1)}, u32[]{:S(2)}, u32[]{:S(2)}) collective-permute-start(bf16[392,128]{1,0:T(8,128)(2,1)S(1)} %get-tuple-element.28), channel_id=1, source_target_pairs={{0,2},{2,0},{4,6},{6,4},{8,10},{10,8},{12,14},{14,12},{1,3},{3,1},... | collective-permute-start | bytes 301064 | tf_op jit(solution)/shard_map/ppermute | solution.py:325
  13.6 1.3 %collective-permute-start.6 = (bf16[392,128]{1,0:T(8,128)(2,1)S(1)}, bf16[392,128]{1,0:T(8,128)(2,1)S(1)}, u32[]{:S(2)}, u32[]{:S(2)}) collective-permute-start(bf16[392,128]{1,0:T(8,128)(2,1)S(1)} %get-tuple-element.29), channel_id=1, source_target_pairs={{0,12},{2,14},{4,8},{6,10},{8,4},{10,6},{12,0},{14,2},{1,13},{3,15... | collective-permute-start | bytes 301064 | tf_op jit(solution)/shard_map/ppermute | solution.py:325
  15.0 0.2 collective-permute-start.2
  15.2 3.9 %collective-permute-start.7 = (bf16[392,128]{1,0:T(8,128)(2,1)S(1)}, bf16[392,128]{1,0:T(8,128)(2,1)S(1)}, u32[]{:S(2)}, u32[]{:S(2)}) collective-permute-start(bf16[392,128]{1,0:T(8,128)(2,1)S(1)} %get-tuple-element.30), channel_id=1, source_target_pairs={{0,14},{2,12},{4,10},{6,8},{8,6},{10,4},{12,2},{14,0},{1,15},{3,13... | collective-permute-start | bytes 301064 | tf_op jit(solution)/shard_map/ppermute | solution.py:325
  19.1 1.4 %shard_map.55.refs_0_ = bf16[392,128]{1,0:T(8,128)(2,1)S(1)} custom-call(s32[3]{0:T(128)S(1)} %copy-done, s32[3]{0:T(128)S(1)} %bitcast.4, bf16[384,4096]{1,0:T(8,128)(2,1)S(1)} %collective-permute-done.x_ref, f32[64,128]{1,0:T(8,128)S(1)} %get-tuple-element.22.g_ref, bf16[4096,512]{1,0:T(8,128)(2,1)S(1)} %get-tuple-element.23.w_ref, ...), custom_call_target="tpu_custom_call" | custom-call | flops 402653184 | bytes 5177344 | tf_op jit(solution)/shard_map/pallas_call | solution.py:210
  20.5 1.8 %collective-permute-start.3 = (bf16[392,128]{1,0:T(8,128)(2,1)S(1)}, bf16[392,128]{1,0:T(8,128)(2,1)S(1)}, u32[]{:S(2)}, u32[]{:S(2)}) collective-permute-start(bf16[392,128]{1,0:T(8,128)(2,1)S(1)} %get-tuple-element.30), channel_id=1, source_target_pairs={{0,6},{2,4},{4,2},{6,0},{8,14},{10,12},{12,10},{14,8},{1,7},{3,5},... | collective-permute-start | bytes 301064 | tf_op jit(solution)/shard_map/ppermute | solution.py:325
  22.4 4.1 %collective-permute-start.4 = (bf16[392,128]{1,0:T(8,128)(2,1)S(1)}, bf16[392,128]{1,0:T(8,128)(2,1)S(1)}, u32[]{:S(2)}, u32[]{:S(2)}) collective-permute-start(bf16[392,128]{1,0:T(8,128)(2,1)S(1)} %shard_map.55.refs_0_), channel_id=1, source_target_pairs={{0,8},{2,10},{4,12},{6,14},{8,0},{10,2},{12,4},{14,6},{1,9},{3,11}... | collective-permute-start | bytes 301064 | tf_op jit(solution)/shard_map/ppermute | solution.py:325
  26.5 0.5 %collective-permute-done.3.refs_3_ = bf16[392,128]{1,0:T(8,128)(2,1)S(1)} collective-permute-done((bf16[392,128]{1,0:T(8,128)(2,1)S(1)}, bf16[392,128]{1,0:T(8,128)(2,1)S(1)}, u32[]{:S(2)}, u32[]{:S(2)}) %collective-permute-start.3) | collective-permute-done | bytes 100384 | tf_op jit(solution)/shard_map/ppermute | solution.py:325
  27.0 4.8 %collective-permute-done.4.refs_4_ = bf16[392,128]{1,0:T(8,128)(2,1)S(1)} collective-permute-done((bf16[392,128]{1,0:T(8,128)(2,1)S(1)}, bf16[392,128]{1,0:T(8,128)(2,1)S(1)}, u32[]{:S(2)}, u32[]{:S(2)}) %collective-permute-start.4) | collective-permute-done | bytes 100384 | tf_op jit(solution)/shard_map/ppermute | solution.py:325
  31.8 0.2 route.1
  32.0 0.4 collective-permute-start.9
  32.4 1.1 %collective-permute-start.10 = (bf16[8,4,32,128]{3,2,1,0:T(8,128)(2,1)S(1)}, bf16[8,4,32,128]{3,2,1,0:T(8,128)(2,1)S(1)}, u32[]{:S(2)}, u32[]{:S(2)}) collective-permute-start(bf16[8,4,32,128]{3,2,1,0:T(8,128)(2,1)S(1)} %get-tuple-element.34), channel_id=1, source_target_pairs={{0,4},{2,6},{4,0},{6,2},{8,12},{10,14},{12,8},{14,10},{1,5},{3,7},... | collective-permute-start | bytes 786440 | tf_op jit(solution)/shard_map/ppermute | solution.py:325
  33.6 2.0 %collective-permute-start.8 = (bf16[8,4,32,128]{3,2,1,0:T(8,128)(2,1)S(1)}, bf16[8,4,32,128]{3,2,1,0:T(8,128)(2,1)S(1)}, u32[]{:S(2)}, u32[]{:S(2)}) collective-permute-start(bf16[8,4,32,128]{3,2,1,0:T(8,128)(2,1)S(1)} %get-tuple-element.31), channel_id=1, source_target_pairs={{0,6},{2,4},{4,2},{6,0},{8,14},{10,12},{12,10},{14,8},{1,7},{3,5},... | collective-permute-start | bytes 786440 | tf_op jit(solution)/shard_map/ppermute | solution.py:325
  35.6 4.8 %collective-permute-done.9.refs_1_ = bf16[8,4,32,128]{3,2,1,0:T(8,128)(2,1)S(1)} collective-permute-done((bf16[8,4,32,128]{3,2,1,0:T(8,128)(2,1)S(1)}, bf16[8,4,32,128]{3,2,1,0:T(8,128)(2,1)S(1)}, u32[]{:S(2)}, u32[]{:S(2)}) %collective-permute-start.9) | collective-permute-done | bytes 262176 | tf_op jit(solution)/shard_map/ppermute | solution.py:325
  40.4 1.3 %collective-permute-done.10.refs_2_ = bf16[8,4,32,128]{3,2,1,0:T(8,128)(2,1)S(1)} collective-permute-done((bf16[8,4,32,128]{3,2,1,0:T(8,128)(2,1)S(1)}, bf16[8,4,32,128]{3,2,1,0:T(8,128)(2,1)S(1)}, u32[]{:S(2)}, u32[]{:S(2)}) %collective-permute-start.10) | collective-permute-done | bytes 262176 | tf_op jit(solution)/shard_map/ppermute | solution.py:325
  41.6 1.0 %join.1.refs_1_ = bf16[8,128,512]{2,1,0:T(8,128)(2,1)} custom-call(bf16[8,4,32,128]{3,2,1,0:T(8,128)(2,1)S(1)} %get-tuple-element.32.refs_0_, bf16[8,4,32,128]{3,2,1,0:T(8,128)(2,1)S(1)} %collective-permute-done.9.refs_1_, bf16[8,4,32,128]{3,2,1,0:T(8,128)(2,1)S(1)} %collective-permute-done.10.refs_2_), custom_call_target="tpu_custom_call" | custom-call | bytes 1572864 | tf_op jit(solution)/shard_map/join/pallas_call | solution.py:303
  42.6 4.1 %collective-permute-done.8.refs_0_ = bf16[8,4,32,128]{3,2,1,0:T(8,128)(2,1)S(1)} collective-permute-done((bf16[8,4,32,128]{3,2,1,0:T(8,128)(2,1)S(1)}, bf16[8,4,32,128]{3,2,1,0:T(8,128)(2,1)S(1)}, u32[]{:S(2)}, u32[]{:S(2)}) %collective-permute-start.8) | collective-permute-done | bytes 262176 | tf_op jit(solution)/shard_map/ppermute | solution.py:325
  46.7 0.7 %join_last.1 = bf16[8,128,512]{2,1,0:T(8,128)(2,1)} custom-call(bf16[8,4,32,128]{3,2,1,0:T(8,128)(2,1)S(1)} %collective-permute-done.8.refs_0_, bf16[8,128,512]{2,1,0:T(8,128)(2,1)} %join.1.refs_1_), custom_call_target="tpu_custom_call", output_to_operand_aliasing={{}: (1, {})} | custom-call | bytes 524288 | tf_op jit(solution)/shard_map/join_last/pallas_call | solution.py:303
  (9 shorter events, 0.0 us)
Async XLA Ops:
  0.0 6.0 %collective-permute-start = (bf16[384,4096]{1,0:T(8,128)(2,1)}, bf16[384,4096]{1,0:T(8,128)(2,1)S(1)}, u32[]{:S(2)}, u32[]{:S(2)}) collective-permute-start(bf16[384,4096]{1,0:T(8,128)(2,1)} %bitcast.5), channel_id=1, source_target_pairs={{0,1},{1,0},{2,3},{3,2},{4,5},{5,4},{6,7},{7,6},{8,9},{9,8},{10,11... | collective-permute-start | bytes 9437192 | tf_op jit(solution)/shard_map/ppermute | solution.py:322
  0.5 5.5 %copy-start = (s32[3]{0:T(128)S(1)}, s32[3]{0:T(128)}, u32[]{:S(2)}) copy-start(s32[3]{0:T(128)} %len_ref.3) | copy-start | bytes 40
  0.5 5.5 %copy-start.1 = (s32[3,1]{0,1:T(1,128)S(1)}, s32[3,1]{0,1:T(1,128)}, u32[]{:S(2)}) copy-start(s32[3,1]{0,1:T(1,128)} %param.9) | copy-start | bytes 40
  8.1 12.4 %collective-permute-start.5 = (bf16[392,128]{1,0:T(8,128)(2,1)S(1)}, bf16[392,128]{1,0:T(8,128)(2,1)S(1)}, u32[]{:S(2)}, u32[]{:S(2)}) collective-permute-start(bf16[392,128]{1,0:T(8,128)(2,1)S(1)} %get-tuple-element.28), channel_id=1, source_target_pairs={{0,10},{2,8},{4,14},{6,12},{8,2},{10,0},{12,6},{14,4},{1,11},{3,9}... | collective-permute-start | bytes 301064 | tf_op jit(solution)/shard_map/ppermute | solution.py:325
  13.1 9.3 %collective-permute-start.1 = (bf16[392,128]{1,0:T(8,128)(2,1)S(1)}, bf16[392,128]{1,0:T(8,128)(2,1)S(1)}, u32[]{:S(2)}, u32[]{:S(2)}) collective-permute-start(bf16[392,128]{1,0:T(8,128)(2,1)S(1)} %get-tuple-element.28), channel_id=1, source_target_pairs={{0,2},{2,0},{4,6},{6,4},{8,10},{10,8},{12,14},{14,12},{1,3},{3,1},... | collective-permute-start | bytes 301064 | tf_op jit(solution)/shard_map/ppermute | solution.py:325
  13.6 12.9 %collective-permute-start.6 = (bf16[392,128]{1,0:T(8,128)(2,1)S(1)}, bf16[392,128]{1,0:T(8,128)(2,1)S(1)}, u32[]{:S(2)}, u32[]{:S(2)}) collective-permute-start(bf16[392,128]{1,0:T(8,128)(2,1)S(1)} %get-tuple-element.29), channel_id=1, source_target_pairs={{0,12},{2,14},{4,8},{6,10},{8,4},{10,6},{12,0},{14,2},{1,13},{3,15... | collective-permute-start | bytes 301064 | tf_op jit(solution)/shard_map/ppermute | solution.py:325
  15.0 11.5 %collective-permute-start.2 = (bf16[392,128]{1,0:T(8,128)(2,1)S(1)}, bf16[392,128]{1,0:T(8,128)(2,1)S(1)}, u32[]{:S(2)}, u32[]{:S(2)}) collective-permute-start(bf16[392,128]{1,0:T(8,128)(2,1)S(1)} %get-tuple-element.29), channel_id=1, source_target_pairs={{0,4},{2,6},{4,0},{6,2},{8,12},{10,14},{12,8},{14,10},{1,5},{3,7},... | collective-permute-start | bytes 301064 | tf_op jit(solution)/shard_map/ppermute | solution.py:325
  15.2 11.3 %collective-permute-start.7 = (bf16[392,128]{1,0:T(8,128)(2,1)S(1)}, bf16[392,128]{1,0:T(8,128)(2,1)S(1)}, u32[]{:S(2)}, u32[]{:S(2)}) collective-permute-start(bf16[392,128]{1,0:T(8,128)(2,1)S(1)} %get-tuple-element.30), channel_id=1, source_target_pairs={{0,14},{2,12},{4,10},{6,8},{8,6},{10,4},{12,2},{14,0},{1,15},{3,13... | collective-permute-start | bytes 301064 | tf_op jit(solution)/shard_map/ppermute | solution.py:325
  20.5 6.5 %collective-permute-start.3 = (bf16[392,128]{1,0:T(8,128)(2,1)S(1)}, bf16[392,128]{1,0:T(8,128)(2,1)S(1)}, u32[]{:S(2)}, u32[]{:S(2)}) collective-permute-start(bf16[392,128]{1,0:T(8,128)(2,1)S(1)} %get-tuple-element.30), channel_id=1, source_target_pairs={{0,6},{2,4},{4,2},{6,0},{8,14},{10,12},{12,10},{14,8},{1,7},{3,5},... | collective-permute-start | bytes 301064 | tf_op jit(solution)/shard_map/ppermute | solution.py:325
  22.4 9.4 %collective-permute-start.4 = (bf16[392,128]{1,0:T(8,128)(2,1)S(1)}, bf16[392,128]{1,0:T(8,128)(2,1)S(1)}, u32[]{:S(2)}, u32[]{:S(2)}) collective-permute-start(bf16[392,128]{1,0:T(8,128)(2,1)S(1)} %shard_map.55.refs_0_), channel_id=1, source_target_pairs={{0,8},{2,10},{4,12},{6,14},{8,0},{10,2},{12,4},{14,6},{1,9},{3,11}... | collective-permute-start | bytes 301064 | tf_op jit(solution)/shard_map/ppermute | solution.py:325
  32.0 8.3 %collective-permute-start.9 = (bf16[8,4,32,128]{3,2,1,0:T(8,128)(2,1)S(1)}, bf16[8,4,32,128]{3,2,1,0:T(8,128)(2,1)S(1)}, u32[]{:S(2)}, u32[]{:S(2)}) collective-permute-start(bf16[8,4,32,128]{3,2,1,0:T(8,128)(2,1)S(1)} %get-tuple-element.33), channel_id=1, source_target_pairs={{0,2},{2,0},{4,6},{6,4},{8,10},{10,8},{12,14},{14,12},{1,3},{3,1},... | collective-permute-start | bytes 786440 | tf_op jit(solution)/shard_map/ppermute | solution.py:325
  32.4 9.2 %collective-permute-start.10 = (bf16[8,4,32,128]{3,2,1,0:T(8,128)(2,1)S(1)}, bf16[8,4,32,128]{3,2,1,0:T(8,128)(2,1)S(1)}, u32[]{:S(2)}, u32[]{:S(2)}) collective-permute-start(bf16[8,4,32,128]{3,2,1,0:T(8,128)(2,1)S(1)} %get-tuple-element.34), channel_id=1, source_target_pairs={{0,4},{2,6},{4,0},{6,2},{8,12},{10,14},{12,8},{14,10},{1,5},{3,7},... | collective-permute-start | bytes 786440 | tf_op jit(solution)/shard_map/ppermute | solution.py:325
  33.6 13.2 %collective-permute-start.8 = (bf16[8,4,32,128]{3,2,1,0:T(8,128)(2,1)S(1)}, bf16[8,4,32,128]{3,2,1,0:T(8,128)(2,1)S(1)}, u32[]{:S(2)}, u32[]{:S(2)}) collective-permute-start(bf16[8,4,32,128]{3,2,1,0:T(8,128)(2,1)S(1)} %get-tuple-element.31), channel_id=1, source_target_pairs={{0,6},{2,4},{4,2},{6,0},{8,14},{10,12},{12,10},{14,8},{1,7},{3,5},... | collective-permute-start | bytes 786440 | tf_op jit(solution)/shard_map/ppermute | solution.py:325
